TPU v7x, 256 devices: a whole 4x4x8 slice. The times are simulated.
256 devices in a mesh: pole: 4 (over y), row: 8 (over z), col: 8 (over x, core).
Axes of the slice: x: 4, y: 4, z: 8, core: 2. Of those that a mesh axis runs over, the one named last changes fastest.
Arguments:
- root_inverse: float32 [8, 1024, 1024], P('pole', ('row', 'col')), may hold values from -100 to 100
- node_factor: float32 [8, 8, 1024, 512], P('pole', 'row', None, 'col'), may hold values from -0.1875 to 0.1875
- node_inverse: float32 [8, 8, 512, 512], P('pole', 'row'), may hold values from -100 to 100
- leaf_root_factor: float32 [8, 64, 1024, 256], P('pole', ('row', 'col')), may hold values from -0.1875 to 0.1875
- leaf_node_factor: float32 [8, 64, 512, 256], P('pole', ('row', 'col')), may hold values from -0.25 to 0.25
- leaf_inverse: float32 [8, 64, 256, 256], P('pole', ('row', 'col')), may hold values from -100 to 100
- leaf_pattern: int32 [64, 8], P(('row', 'col')), may hold values 0 or 1
- pole_weight: float32 [8], P('pole'), may hold values from 0.1 to 1
Outputs:
- root_block: float32 [1024, 1024], P(('row', 'col'))
- node_offdiag: float32 [8, 1024, 512], P('row', None, 'col')
- node_diag: float32 [8, 512, 512], P('row', 'col')
- leaf_root: float32 [64, 1024, 256], P(('row', 'col'))
- leaf_node: float32 [64, 512, 256], P(('row', 'col'))
- leaf_diag: float32 [64, 256, 256], P(('row', 'col'))
All inputs are finite; a program needn't handle non-finite values. No bound on the sum of `leaf_pattern` on one device may be relied on, other than what follows from the above.
Results may differ from a plain program's by a relative error of at most 0.0001.
Values sent between devices are 32-bit elements; how exact they have to be, the bound alone decides.
A program may use at most 64 MiB of HBM per device.

v0:
```python
import jax
import jax.numpy as jnp
from jax import lax
from jax.sharding import PartitionSpec as P

highest = lax.Precision.HIGHEST


def product(left, right):
    return jnp.matmul(left, right, precision=highest)


def weighted(weights, values):
    return jnp.sum(weights[:, None, None] * values, axis=0)


def shards(
    root_inverse,
    node_factor,
    node_inverse,
    leaf_root_factor,
    leaf_node_factor,
    leaf_inverse,
    leaf_pattern,
    pole_weight,
):
    node_cols = node_factor[:, 0]
    node_inv = node_inverse[:, 0]
    node_leaf = leaf_node_factor[:, 0]
    leaf_inv = leaf_inverse[:, 0]
    block_rows = leaf_root_factor.shape[2] // leaf_pattern.shape[1]
    row_mask = jnp.repeat(leaf_pattern[0].astype(jnp.float32), block_rows)
    root_leaf = leaf_root_factor[:, 0] * row_mask[None, :, None]
    width = node_cols.shape[2]
    joined = jnp.concatenate([node_cols, root_leaf], axis=2)
    products = product(lax.all_gather(root_inverse, ("row", "col"), axis=1, tiled=True), joined)
    offdiag = -products[:, :, :width]
    root_times = products[:, :, width:]
    col_index = lax.axis_index("col")
    own_rows = lax.dynamic_slice_in_dim(node_inv, col_index * width, width, 1)
    factor_t = jnp.swapaxes(node_cols, 1, 2)
    piece = lax.all_gather(offdiag, "col", axis=2, tiled=True)
    root_sum = root_times
    root_sum = root_sum + product(piece, node_leaf)
    node_part = product(jnp.swapaxes(piece, 1, 2), root_leaf)
    cross = product(factor_t, piece)
    root_sum, node_part, cross = (root_sum, node_part, cross)
    diag_rows = own_rows - cross
    diag_times = product(lax.all_gather(diag_rows, "col", axis=1, tiled=True), node_leaf)
    upper_levels = (
        weighted(pole_weight, root_inverse),
        weighted(pole_weight, offdiag)[None],
        weighted(pole_weight, diag_rows)[None],
    )
    middle_part = node_part + diag_times
    lower_part = (
        leaf_inv
        + product(jnp.swapaxes(root_leaf, 1, 2), root_sum)
        + product(jnp.swapaxes(node_leaf, 1, 2), middle_part)
    )
    leaf_levels = (
        weighted(pole_weight, -root_sum)[None],
        weighted(pole_weight, -middle_part)[None],
        weighted(pole_weight, lower_part)[None],
    )
    totals = lax.psum(
        (
            upper_levels[0],
            upper_levels[1],
            upper_levels[2],
            leaf_levels[0],
            leaf_levels[1],
            leaf_levels[2],
        ),
        "pole",
    )
    return (totals[0], totals[1], totals[2], totals[3], totals[4], totals[5])


def solution(mesh):
    return jax.shard_map(
        shards,
        mesh=mesh,
        in_specs=(
            P("pole", ("row", "col"), None),
            P("pole", "row", None, "col"),
            P("pole", "row", None, None),
            P("pole", ("row", "col"), None, None),
            P("pole", ("row", "col"), None, None),
            P("pole", ("row", "col"), None, None),
            P(("row", "col"), None),
            P("pole"),
        ),
        out_specs=(
            P(("row", "col"), None),
            P("row", None, "col"),
            P("row", "col", None),
            P(("row", "col"), None, None),
            P(("row", "col"), None, None),
            P(("row", "col"), None, None),
        ),
        check_vma=False,
    )
```

profile of v0, /device:TPU:1, one launch (start us, length us, event | category | flops | bytes accessed | tf_op | source)
XLA Modules:
  0.0 272.0 jit_solution(6661913665170530114)
XLA Ops:
  7.2 0.0 copy-start
  7.2 0.0 all-gather.4.cloned.1.call-start
  7.2 0.7 all-gather.4.cloned.1.call-update
  7.9 0.0 copy-start.12
  7.9 0.0 all-gather.6.cloned.1.call-start
  8.0 2.9 %copy.20 = f32[2,1,1024,256]{2,3,0,1:T(8,128)} copy(f32[2,1,1024,256]{3,2,1,0:T(8,128)} %param.11) | data formatting | bytes 4194304 | tf_op args[3]
  10.9 0.0 copy-done.12
  10.9 0.1 broadcast_bitcast_fusion
  11.0 1.8 bitcast_multiply_fusion
  12.8 85.2 %all-gather.4.cloned.1.call-done = f32[2,1024,1024]{2,1,0:T(8,128)} async-done(((f32[2,16,1024]{2,1,0:T(8,128)}), f32[2,1024,1024]{2,1,0:T(8,128)}) %all-gather.4.cloned.1.call-update) | async-done | bytes 8388624 | tf_op jit(solution)/shard_map/all_gather | solution.py:36
  98.0 11.3 %fusion.4 = f32[2,1024,320]{1,2,0:T(8,128)S(1)} fusion(f32[2,1024,1024]{2,1,0:T(8,128)} %all-gather.4.cloned.1.call-done, f32[2,1024,256]{1,2,0:T(8,128)S(1)} %bitcast_multiply_fusion, f32[2,1024,64]{1,2,0:T(8,128)} %bitcast.54), kind=kOutput, calls=%fused_computation.7 | convolution fusion | flops 8053719040 | bytes 13631488 | tf_op jit(solution)/shard_map/dot_general | solution.py:10
  109.4 0.0 copy-start.2
  109.4 1.5 copy-done.2
  110.9 0.0 copy-done.11
  110.9 1.6 slice_negate_fusion
  112.5 0.0 all-gather.6.cloned.1.call-update
  112.5 0.0 all-gather.8.cloned.1.call-start
  112.5 0.0 copy-start.6
  112.5 31.9 %all-gather.6.cloned.1.call-done = f32[2,1024,512]{1,2,0:T(8,128)} async-done(((f32[2,1024,64]{1,2,0:T(8,128)}), f32[2,1024,512]{1,2,0:T(8,128)}) %all-gather.6.cloned.1.call-update) | async-done | bytes 4194320 | tf_op jit(solution)/shard_map/all_gather | solution.py:42
  144.5 7.9 %multiply_reduce_fusion.3 = (f32[64,512]{1,0:T(8,128)}, f32[2,64,512]{2,1,0:T(8,128)}) fusion(f32[2]{0:T(128)S(1)} %copy-done.11, f32[2,1024,512]{1,2,0:T(8,128)} %all-gather.6.cloned.1.call-done, f32[2,1,1024,64]{2,3,1,0:T(8,128)} %param.9, f32[2,1,512,512]{3,2,1,0:T(8,128)} %param.10, s32[]{:T(128)S(6)} %select_n.3), kind=kOutput, calls=%fused_computation.23 | convolution fusion | flops 805470208 | bytes 5373964 | tf_op jit(solution)/shard_map/dot_general | solution.py:10
  152.4 0.0 all-gather.8.cloned.1.call-update
  152.4 0.2 all-reduce.3.cloned.1.call-start
  152.6 0.0 copy-done.6
  152.6 0.7 multiply_reduce_fusion.4
  153.3 0.0 copy-done
  153.3 8.0 %multiply_reduce_fusion = (f32[1024,256]{0,1:T(8,128)}, f32[2,1024,256]{1,2,0:T(8,128)S(1)}) fusion(f32[2]{0:T(128)S(1)} %copy-done.11, f32[2,1024,512]{1,2,0:T(8,128)} %all-gather.6.cloned.1.call-done, f32[2,1,512,256]{3,2,1,0:T(8,128)S(1)} %copy-done, f32[2,1024,320]{1,2,0:T(8,128)} %copy-done.2), kind=kOutput, calls=%fused_computation.6 | convolution fusion | flops 3223060480 | bytes 10485768 | tf_op jit(solution)/shard_map/dot_general | solution.py:10
  161.3 0.0 copy-done.4
  161.3 2.9 %convolution_add_fusion.1 = f32[2,256,256]{2,1,0:T(8,128)} fusion(f32[2,1024,256]{1,2,0:T(8,128)S(1)} %bitcast_multiply_fusion, f32[2,1024,256]{1,2,0:T(8,128)S(1)} %get-tuple-element.23, f32[2,1,256,256]{3,2,1,0:T(8,128)S(1)} %copy-done.4), kind=kOutput, calls=%fused_computation.11 | convolution fusion | flops 1610743808 | bytes 5242880 | tf_op jit(solution)/shard_map/dot_general | solution.py:10
  164.2 16.0 %all-gather.8.cloned.1.call-done = f32[2,512,512]{2,1,0:T(8,128)} async-done(((f32[2,64,512]{2,1,0:T(8,128)}), f32[2,512,512]{2,1,0:T(8,128)}) %all-gather.8.cloned.1.call-update) | async-done | bytes 2097168 | tf_op jit(solution)/shard_map/all_gather | solution.py:49
  180.2 3.7 %fusion.12 = f32[2,512,256]{2,1,0:T(8,128)S(1)} fusion(f32[2,512,512]{2,1,0:T(8,128)} %all-gather.8.cloned.1.call-done, f32[2,1,512,256]{3,2,1,0:T(8,128)S(1)} %copy-done), kind=kOutput, calls=%fused_computation.17 | convolution fusion | flops 1610612736 | bytes 4194304 | tf_op jit(solution)/shard_map/dot_general | solution.py:10
  184.0 0.0 copy-done.1
  184.0 0.0 copy-start.3
  184.0 4.7 %multiply_reduce_fusion.1 = (f32[512,256]{1,0:T(8,128)}, f32[2,512,256]{2,1,0:T(8,128)S(1)}) fusion(f32[2]{0:T(128)S(1)} %copy-done.11, f32[2,512,256]{2,1,0:T(8,128)S(1)} %fusion.12, f32[2,1024,512]{1,2,0:T(8,128)S(1)} %copy-done.1, f32[2,1024,256]{1,2,0:T(8,128)S(1)} %bitcast_multiply_fusion), kind=kOutput, calls=%fused_computation.20 | convolution fusion | flops 3222142976 | bytes 8912904 | tf_op jit(solution)/shard_map/dot_general | solution.py:10
  188.6 0.0 copy-done.3
  188.7 2.6 fusion.9
  191.2 0.0 all-reduce.3.cloned.1.call-update
  191.2 68.0 %all-reduce.3.cloned.1.call-done = (f32[16,1024]{1,0:T(8,128)}, f32[1,1024,64]{1,2,0:T(8,128)}, f32[1,64,512]{2,1,0:T(8,128)}, f32[1,1024,256]{1,2,0:T(8,128)}, ...) async-done(((f32[16,1024]{1,0:T(8,128)}, f32[1,1024,64]{1,2,0:T(8,128)}, f32[1,64,512]{2,1,0:T(8,128)}, f32[1,1024,256]{1,2,0:T(8,128)}, f32[1,512,256]{2,1,0:T(8,128)}, ...) | async-done | bytes 2293776 | tf_op jit(solution)/shard_map/psum | solution.py:66
  259.3 2.6 copy.26
  261.9 0.0 copy-done.10
  261.9 0.6 copy.38
  262.6 0.0 copy-done.8
  262.6 0.7 copy.39
  263.3 0.0 copy-done.9
  263.3 0.7 copy.40
  263.9 0.0 copy-done.5
  263.9 0.8 copy.41
  264.7 0.0 copy-done.7
  264.7 0.7 copy.42
  (9 shorter events, 0.0 us)
Async XLA Ops:
  7.2 146.2 %copy-start = (f32[2,1,512,256]{3,2,1,0:T(8,128)S(1)}, f32[2,1,512,256]{3,2,1,0:T(8,128)}, u32[]{:S(2)}) copy-start(f32[2,1,512,256]{3,2,1,0:T(8,128)} %param.12) | copy-start | bytes 3145732
  7.2 90.8 %all-gather.4.cloned.1.call-start = ((), (), s32[]{:S(2)}) async-start(), calls=%async_computation | async-start | bytes 8519680 | tf_op jit(solution)/shard_map/all_gather | solution.py:36
  7.9 3.0 %copy-start.12 = (s32[1,8]{1,0:T(1,128)S(1)}, s32[1,8]{1,0:T(1,128)}, u32[]{:S(2)}) copy-start(s32[1,8]{1,0:T(1,128)} %param.14) | copy-start | bytes 100
  7.9 136.6 %all-gather.6.cloned.1.call-start = ((), (), s32[]{:S(2)}) async-start(), calls=%async_computation.1 | async-start | bytes 4718592 | tf_op jit(solution)/shard_map/all_gather | solution.py:42
  98.0 12.9 %copy-start.11 = (f32[2]{0:T(128)S(1)}, f32[2]{0:T(128)}, u32[]{:S(2)}) copy-start(f32[2]{0:T(128)} %param.15) | copy-start | bytes 28
  109.4 1.5 copy-start.2
  112.5 67.8 %all-gather.8.cloned.1.call-start = ((), (), s32[]{:S(2)}) async-start(), calls=%async_computation.2 | async-start | bytes 2359296 | tf_op jit(solution)/shard_map/all_gather | solution.py:49
  112.5 40.1 %copy-start.6 = (f32[2,16,1024]{2,1,0:T(8,128)S(1)}, f32[2,16,1024]{2,1,0:T(8,128)}, u32[]{:S(2)}) copy-start(f32[2,16,1024]{2,1,0:T(8,128)} %param.8) | copy-start | bytes 393220
  152.4 106.9 %all-reduce.3.cloned.1.call-start = ((), (), s32[]{:S(2)}) async-start(), calls=%async_computation.3 | async-start | bytes 4587520 | tf_op jit(solution)/shard_map/psum | solution.py:66
  153.3 8.0 %copy-start.4 = (f32[2,1,256,256]{3,2,1,0:T(8,128)S(1)}, f32[2,1,256,256]{3,2,1,0:T(8,128)}, u32[]{:S(2)}) copy-start(f32[2,1,256,256]{3,2,1,0:T(8,128)} %param.13) | copy-start | bytes 1572868
  180.2 3.7 %copy-start.1 = (f32[2,1024,512]{1,2,0:T(8,128)S(1)}, f32[2,1024,512]{1,2,0:T(8,128)}, u32[]{:S(2)}) copy-start(f32[2,1024,512]{1,2,0:T(8,128)} %all-gather.6.cloned.1.call-done) | copy-start | bytes 12582916
  184.0 4.7 %copy-start.3 = (f32[2,256,256]{2,1,0:T(8,128)S(1)}, f32[2,256,256]{2,1,0:T(8,128)}, u32[]{:S(2)}) copy-start(f32[2,256,256]{2,1,0:T(8,128)} %convolution_add_fusion.1) | copy-start | bytes 1572868
  259.3 2.6 copy-start.10
  259.3 3.3 %copy-start.8 = (f32[1,1024,64]{1,2,0:T(8,128)S(1)}, f32[1,1024,64]{1,2,0:T(8,128)}, u32[]{:S(2)}) copy-start(f32[1,1024,64]{1,2,0:T(8,128)} %get-tuple-element.27) | copy-start | bytes 786436
  259.3 4.0 %copy-start.9 = (f32[1,64,512]{2,1,0:T(8,128)S(1)}, f32[1,64,512]{2,1,0:T(8,128)}, u32[]{:S(2)}) copy-start(f32[1,64,512]{2,1,0:T(8,128)} %get-tuple-element.28) | copy-start | bytes 393220
  259.3 4.6 %copy-start.5 = (f32[1,512,256]{2,1,0:T(8,128)S(1)}, f32[1,512,256]{2,1,0:T(8,128)}, u32[]{:S(2)}) copy-start(f32[1,512,256]{2,1,0:T(8,128)} %get-tuple-element.30) | copy-start | bytes 1572868
  259.3 5.4 %copy-start.7 = (f32[1,256,256]{2,1,0:T(8,128)S(1)}, f32[1,256,256]{2,1,0:T(8,128)}, u32[]{:S(2)}) copy-start(f32[1,256,256]{2,1,0:T(8,128)} %get-tuple-element.31) | copy-start | bytes 786436
Sparse Core Ops, SparseCore 0:
  10.8 87.1 all-gather.3
  112.6 31.8 all-gather.5
  152.5 27.6 all-gather.7
  191.4 67.8 all-reduce.2
where the time goes:
time: 272 us
  waiting for transfers between devices  202 us (74%)
  matrix products  41 us (15%)
  between operations  13.9 us (5%)
  local copies, waits for them, and re-layouts  10.7 us (4%)
  other arithmetic  4.09 us (2%)
    all_gather x1, waiting for transfers between devices, shards(): lax.all_gather(root_inverse, ('row', 'col'), axis=1, tiled=True)  85.2 us
    psum x1, waiting for transfers between devices, shards(): lax.psum((upper_levels[0], upper_levels[1], upper_levels[2], leaf_levels[...  68 us
    dot_general x7, matrix products, product(): return jnp.matmul(left, right, precision=highest)  41 us
    all_gather x1, waiting for transfers between devices, shards(): piece = lax.all_gather(offdiag, 'col', axis=2, tiled=True)  31.9 us
    all_gather x1, waiting for transfers between devices, shards(): lax.all_gather(diag_rows, 'col', axis=1, tiled=True)  16 us
    unnamed x33, local copies, waits for them, and re-layouts  10.6 us
  transfers between devices with their start and end apart: 4, of which 4 were waited for; matrix products, arithmetic and copies ran while one was open for 6% of the time, Pallas kernels for 0%

commit v1 on v0

--- a/solution.py
+++ b/solution.py
@@ -4,6 +4,11 @@
 from jax.sharding import PartitionSpec as P
 
 highest = lax.Precision.HIGHEST
+
+
+def all_by_exchange(x, axis, d):
+    sent = jnp.stack([x] * lax.axis_size(axis))
+    return jnp.concatenate(lax.all_to_all(sent, axis, 0, 0), axis=d)
 
 
 def product(left, right):
@@ -33,7 +38,7 @@
     root_leaf = leaf_root_factor[:, 0] * row_mask[None, :, None]
     width = node_cols.shape[2]
     joined = jnp.concatenate([node_cols, root_leaf], axis=2)
-    products = product(lax.all_gather(root_inverse, ("row", "col"), axis=1, tiled=True), joined)
+    products = product(all_by_exchange(root_inverse, ("row", "col"), 1), joined)
     offdiag = -products[:, :, :width]
     root_times = products[:, :, width:]
     col_index = lax.axis_index("col")

time: 272 us -> 388 us (1.43)
  waiting for transfers between devices: 202 us -> 299 us
  starting transfers between devices: 0.34 us -> 13.6 us
  local copies, waits for them, and re-layouts: 10.7 us -> 19.2 us
    all_to_all x0 -> x1, waiting for transfers between devices: none -> 179 us  [all_by_exchange(): return jnp.concatenate(lax.all_to_all(sent, axis, 0, 0), axis=d)]
    all_gather x1 -> x0, waiting for transfers between devices: 85.2 us -> none  [shards(): lax.all_gather(root_inverse, ('row', 'col'), axis=1, tiled=True)]
    all_to_all x0 -> x1, starting transfers between devices: none -> 13.3 us  [all_by_exchange(): return jnp.concatenate(lax.all_to_all(sent, axis, 0, 0), axis=d)]
    another operation x0 -> x1, local copies, waits for them, and re-layouts: none -> 5.29 us  [all_by_exchange(): sent = jnp.stack([x] * lax.axis_size(axis))]
    reshape x0 -> x1, local copies, waits for them, and re-layouts: none -> 4.29 us  [all_by_exchange(): return jnp.concatenate(lax.all_to_all(sent, axis, 0, 0), axis=d)]
    all_gather x1, waiting for transfers between devices: 31.9 us -> 35.8 us  [shards(): piece = lax.all_gather(offdiag, 'col', axis=2, tiled=True)]
    unnamed x33 -> x37, local copies, waits for them, and re-layouts: 10.6 us -> 9.56 us
  transfers between devices with their start and end apart: 4 -> 4, of which waited for: 4 -> 4; matrix products, arithmetic and copies ran while one was open for 6% -> 4% of each run, Pallas kernels for 0% -> 0%
where the time goes in v1:
time: 388 us
  waiting for transfers between devices  299 us (77%)
  matrix products  38.7 us (10%)
  local copies, waits for them, and re-layouts  19.2 us (5%)
  between operations  13.9 us (4%)
  starting transfers between devices  13.6 us (4%)
  other arithmetic  4.09 us (1%)
    all_to_all x1, waiting for transfers between devices, all_by_exchange(): return jnp.concatenate(lax.all_to_all(sent, axis, 0, 0), axis=d)  179 us
    psum x1, waiting for transfers between devices, shards(): lax.psum((upper_levels[0], upper_levels[1], upper_levels[2], leaf_levels[...  68 us
    dot_general x7, matrix products, product(): return jnp.matmul(left, right, precision=highest)  38.7 us
    all_gather x1, waiting for transfers between devices, shards(): piece = lax.all_gather(offdiag, 'col', axis=2, tiled=True)  35.8 us
    all_gather x1, waiting for transfers between devices, shards(): lax.all_gather(diag_rows, 'col', axis=1, tiled=True)  16.2 us
    all_to_all x1, starting transfers between devices, all_by_exchange(): return jnp.concatenate(lax.all_to_all(sent, axis, 0, 0), axis=d)  13.3 us
    unnamed x37, local copies, waits for them, and re-layouts  9.56 us
  transfers between devices with their start and end apart: 4, of which 4 were waited for; matrix products, arithmetic and copies ran while one was open for 4% of the time, Pallas kernels for 0%

profile of v1, /device:TPU:1, one launch (start us, length us, event | category | flops | bytes accessed | tf_op | source)
XLA Modules:
  0.0 388.2 jit_solution(11563603786192531948)
XLA Ops:
  7.2 0.0 copy-start
  7.2 5.3 %stack.2 = f32[64,2,16,1024]{3,2,1,0:T(8,128)} broadcast(f32[2,16,1024]{2,1,0:T(8,128)} %param.8), dimensions={1,2,3} | broadcast | bytes 8519680 | tf_op jit(solution)/shard_map/stack | solution.py:10
  12.5 13.3 %all-to-all-start = ((f32[64,2,16,1024]{3,2,1,0:T(8,128)}), f32[64,2,16,1024]{3,2,1,0:T(8,128)}, u32[]{:S(2)}, u32[]{:S(2)}) async-start(f32[64,2,16,1024]{3,2,1,0:T(8,128)} %stack.2), calls=%async_computation | async-start | bytes 16777216 | tf_op jit(solution)/shard_map/all_to_all | solution.py:11
  25.8 0.0 copy-start.14
  25.8 0.0 all-gather.3.cloned.1.call-start
  25.9 0.0 copy-done.3
  25.9 1.8 copy.20
  27.7 0.0 copy-done.14
  27.7 0.1 broadcast_bitcast_fusion
  27.8 1.8 bitcast_multiply_fusion
  29.6 178.6 %all-to-all-done = f32[64,2,16,1024]{3,2,1,0:T(8,128)} async-done(((f32[64,2,16,1024]{3,2,1,0:T(8,128)}), f32[64,2,16,1024]{3,2,1,0:T(8,128)}, u32[]{:S(2)}, u32[]{:S(2)}) %all-to-all-start) | async-done | bytes 8388640 | tf_op jit(solution)/shard_map/all_to_all | solution.py:11
  208.2 4.3 %copy.21 = f32[2,64,16,1024]{3,2,1,0:T(8,128)S(1)} copy(f32[2,64,16,1024]{3,2,0,1:T(8,128)} %bitcast.4) | data formatting | bytes 16777216 | tf_op jit(solution)/shard_map/reshape | solution.py:11
  212.5 0.0 copy-done.5
  212.5 0.0 copy-start.13
  212.5 9.0 %fusion.4 = f32[2,1024,320]{1,2,0:T(8,128)S(1)} fusion(f32[2,1024,1024]{2,1,0:T(8,128)S(1)} %bitcast.54, f32[2,1024,256]{1,2,0:T(8,128)S(1)} %bitcast_multiply_fusion, f32[2,1024,64]{1,2,0:T(8,128)S(1)} %bitcast.57), kind=kOutput, calls=%fused_computation.7 | convolution fusion | flops 8053719040 | bytes 13631488 | tf_op jit(solution)/shard_map/dot_general | solution.py:15
  221.5 0.0 copy-start.2
  221.5 1.5 copy-done.2
  223.1 0.0 copy-done.13
  223.1 1.6 slice_negate_fusion
  224.6 0.0 all-gather.3.cloned.1.call-update
  224.7 0.2 all-gather.5.cloned.1.call-start
  224.9 0.0 copy-start.6
  224.9 35.8 %all-gather.3.cloned.1.call-done = f32[2,1024,512]{1,2,0:T(8,128)} async-done(((f32[2,1024,64]{1,2,0:T(8,128)}), f32[2,1024,512]{1,2,0:T(8,128)}) %all-gather.3.cloned.1.call-update) | async-done | bytes 4194320 | tf_op jit(solution)/shard_map/all_gather | solution.py:47
  260.8 7.9 %multiply_reduce_fusion.3 = (f32[64,512]{1,0:T(8,128)}, f32[2,64,512]{2,1,0:T(8,128)}) fusion(f32[2]{0:T(128)S(1)} %copy-done.13, f32[2,1024,512]{1,2,0:T(8,128)} %all-gather.3.cloned.1.call-done, f32[2,1,1024,64]{2,3,1,0:T(8,128)} %param.9, f32[2,1,512,512]{3,2,1,0:T(8,128)} %param.10, s32[]{:T(128)S(6)} %select_n.3), kind=kOutput, calls=%fused_computation.23 | convolution fusion | flops 805470208 | bytes 5373964 | tf_op jit(solution)/shard_map/dot_general | solution.py:15
  268.6 0.0 all-gather.5.cloned.1.call-update
  268.7 0.0 all-reduce.3.cloned.1.call-start
  268.7 0.0 copy-done.6
  268.7 0.7 multiply_reduce_fusion.4
  269.4 0.0 copy-done
  269.4 8.0 %multiply_reduce_fusion = (f32[1024,256]{0,1:T(8,128)}, f32[2,1024,256]{1,2,0:T(8,128)S(1)}) fusion(f32[2]{0:T(128)S(1)} %copy-done.13, f32[2,1024,512]{1,2,0:T(8,128)} %all-gather.3.cloned.1.call-done, f32[2,1,512,256]{3,2,1,0:T(8,128)S(1)} %copy-done, f32[2,1024,320]{1,2,0:T(8,128)} %copy-done.2), kind=kOutput, calls=%fused_computation.6 | convolution fusion | flops 3223060480 | bytes 10485768 | tf_op jit(solution)/shard_map/dot_general | solution.py:15
  277.4 0.0 copy-done.7
  277.4 2.9 convolution_add_fusion.1
  280.3 16.2 %all-gather.5.cloned.1.call-done = f32[2,512,512]{2,1,0:T(8,128)} async-done(((f32[2,64,512]{2,1,0:T(8,128)}), f32[2,512,512]{2,1,0:T(8,128)}) %all-gather.5.cloned.1.call-update) | async-done | bytes 2097168 | tf_op jit(solution)/shard_map/all_gather | solution.py:54
  296.5 3.7 fusion.12
  300.2 0.0 copy-done.1
  300.2 0.0 copy-start.4
  300.2 4.7 %multiply_reduce_fusion.1 = (f32[512,256]{1,0:T(8,128)}, f32[2,512,256]{2,1,0:T(8,128)S(1)}) fusion(f32[2]{0:T(128)S(1)} %copy-done.13, f32[2,512,256]{2,1,0:T(8,128)S(1)} %fusion.12, f32[2,1024,512]{1,2,0:T(8,128)S(1)} %copy-done.1, f32[2,1024,256]{1,2,0:T(8,128)S(1)} %bitcast_multiply_fusion), kind=kOutput, calls=%fused_computation.20 | convolution fusion | flops 3222142976 | bytes 8912904 | tf_op jit(solution)/shard_map/dot_general | solution.py:15
  304.9 0.0 copy-done.4
  304.9 2.6 fusion.9
  307.5 0.0 all-reduce.3.cloned.1.call-update
  307.5 68.0 %all-reduce.3.cloned.1.call-done = (f32[16,1024]{1,0:T(8,128)}, f32[1,1024,64]{1,2,0:T(8,128)}, f32[1,64,512]{2,1,0:T(8,128)}, f32[1,1024,256]{1,2,0:T(8,128)}, ...) async-done(((f32[16,1024]{1,0:T(8,128)}, f32[1,1024,64]{1,2,0:T(8,128)}, f32[1,64,512]{2,1,0:T(8,128)}, f32[1,1024,256]{1,2,0:T(8,128)}, f32[1,512,256]{2,1,0:T(8,128)}, ...) | async-done | bytes 2293776 | tf_op jit(solution)/shard_map/psum | solution.py:71
  375.6 2.6 copy.27
  378.2 0.6 copy.39
  378.8 0.7 copy.40
  379.5 0.7 copy.41
  380.2 0.0 copy-done.8
  380.2 0.8 copy.42
  381.0 0.7 copy.43
  (14 shorter events, 0.0 us)
Async XLA Ops:
  7.2 262.3 %copy-start = (f32[2,1,512,256]{3,2,1,0:T(8,128)S(1)}, f32[2,1,512,256]{3,2,1,0:T(8,128)}, u32[]{:S(2)}) copy-start(f32[2,1,512,256]{3,2,1,0:T(8,128)} %param.12) | copy-start | bytes 3145732
  12.5 13.4 %copy-start.3 = (f32[2,1,1024,256]{3,2,1,0:T(8,128)S(1)}, f32[2,1,1024,256]{3,2,1,0:T(8,128)}, u32[]{:S(2)}) copy-start(f32[2,1,1024,256]{3,2,1,0:T(8,128)} %param.11) | copy-start | bytes 6291460
  12.5 195.7 %all-to-all-start = ((f32[64,2,16,1024]{3,2,1,0:T(8,128)}), f32[64,2,16,1024]{3,2,1,0:T(8,128)}, u32[]{:S(2)}, u32[]{:S(2)}) async-start(f32[64,2,16,1024]{3,2,1,0:T(8,128)} %stack.2), calls=%async_computation | async-start | bytes 16777216 | tf_op jit(solution)/shard_map/all_to_all | solution.py:11
  25.8 1.9 copy-start.14
  25.8 234.9 %all-gather.3.cloned.1.call-start = ((), (), s32[]{:S(2)}) async-start(), calls=%async_computation.1 | async-start | bytes 4718592 | tf_op jit(solution)/shard_map/all_gather | solution.py:47
  208.2 4.3 %copy-start.5 = (f32[2,1,1024,64]{2,3,1,0:T(8,128)S(1)}, f32[2,1,1024,64]{2,3,1,0:T(8,128)}, u32[]{:S(2)}) copy-start(f32[2,1,1024,64]{2,3,1,0:T(8,128)} %param.9) | copy-start | bytes 1572868
  212.5 10.6 %copy-start.13 = (f32[2]{0:T(128)S(1)}, f32[2]{0:T(128)}, u32[]{:S(2)}) copy-start(f32[2]{0:T(128)} %param.15) | copy-start | bytes 28
  221.5 1.5 copy-start.2
  224.7 71.8 %all-gather.5.cloned.1.call-start = ((), (), s32[]{:S(2)}) async-start(), calls=%async_computation.2 | async-start | bytes 2359296 | tf_op jit(solution)/shard_map/all_gather | solution.py:54
  224.9 43.8 %copy-start.6 = (f32[2,16,1024]{2,1,0:T(8,128)S(1)}, f32[2,16,1024]{2,1,0:T(8,128)}, u32[]{:S(2)}) copy-start(f32[2,16,1024]{2,1,0:T(8,128)} %param.8) | copy-start | bytes 393220
  268.7 106.9 %all-reduce.3.cloned.1.call-start = ((), (), s32[]{:S(2)}) async-start(), calls=%async_computation.3 | async-start | bytes 4587520 | tf_op jit(solution)/shard_map/psum | solution.py:71
  269.4 8.0 %copy-start.7 = (f32[2,1,256,256]{3,2,1,0:T(8,128)S(1)}, f32[2,1,256,256]{3,2,1,0:T(8,128)}, u32[]{:S(2)}) copy-start(f32[2,1,256,256]{3,2,1,0:T(8,128)} %param.13) | copy-start | bytes 1572868
  296.5 3.7 copy-start.1
  300.2 4.7 %copy-start.4 = (f32[2,256,256]{2,1,0:T(8,128)S(1)}, f32[2,256,256]{2,1,0:T(8,128)}, u32[]{:S(2)}) copy-start(f32[2,256,256]{2,1,0:T(8,128)} %convolution_add_fusion.1) | copy-start | bytes 1572868
  375.5 2.6 copy-start.12
  375.6 3.3 copy-start.10
  375.6 4.0 %copy-start.11 = (f32[1,64,512]{2,1,0:T(8,128)S(1)}, f32[1,64,512]{2,1,0:T(8,128)}, u32[]{:S(2)}) copy-start(f32[1,64,512]{2,1,0:T(8,128)} %get-tuple-element.28) | copy-start | bytes 393220
  375.6 4.6 %copy-start.8 = (f32[1,512,256]{2,1,0:T(8,128)S(1)}, f32[1,512,256]{2,1,0:T(8,128)}, u32[]{:S(2)}) copy-start(f32[1,512,256]{2,1,0:T(8,128)} %get-tuple-element.30) | copy-start | bytes 1572868
  375.6 5.4 %copy-start.9 = (f32[1,256,256]{2,1,0:T(8,128)S(1)}, f32[1,256,256]{2,1,0:T(8,128)}, u32[]{:S(2)}) copy-start(f32[1,256,256]{2,1,0:T(8,128)} %get-tuple-element.31) | copy-start | bytes 786436
Sparse Core Ops, SparseCore 0:
  224.8 35.9 all-gather.2
  268.8 27.6 all-gather.4
  307.6 67.8 all-reduce.2
